TPU v7x, 32 devices: a whole 2x2x4 slice. The times are simulated.
32 devices in a mesh: gx: 4 (over y, core), gy: 8 (over z, x).
Axes of the slice: x: 2, y: 2, z: 4, core: 2. Of those that a mesh axis runs over, the one named last changes fastest.
Arguments:
- velocity: float32 [3, 32, 64, 128], P(None, 'gx', 'gy'), may hold values from -6 to 6
- viscosity: float32 [32, 64, 128], P('gx', 'gy'), may hold values from 0.02 to 0.16
- forcing: float32 [4, 3, 32, 64, 128], P(None, None, 'gx', 'gy'), may hold values from -6 to 6
- earlier: float32 [60, 3, 32, 64, 128], P(None, None, 'gx', 'gy'), may hold values from -12 to 12
Outputs:
- velocity_out: float32 [3, 32, 64, 128], P(None, 'gx', 'gy')
- basis: float32 [64, 3, 32, 64, 128], P(None, None, 'gx', 'gy')
- factor: float32 [64, 64], replicated
All inputs are finite; a program needn't handle non-finite values.
Results may differ from a plain program's by a relative error of at most 0.000068.
Values sent between devices are 32-bit elements; how exact they have to be, the bound alone decides.
No kernel may reach another device: no remote copies, remote signals or barrier semaphores. Data moves between devices by JAX's collectives and lax.ppermute only.
A program may use at most 64 MiB of HBM per device.

v0:
```python
import jax
import jax.numpy as jnp
from jax import lax
from jax.sharding import PartitionSpec as P


def padded_2(array, sides, width):
    for axis, dim in sides:
        count, length = (lax.axis_size(axis), array.shape[dim])
        up = [(i, (i + 1) % count) for i in range(count - 1)]
        down = [(j, i) for i, j in up]
        last = lax.slice_in_dim(array, length - width, length, axis=dim)
        initial = lax.slice_in_dim(array, 0, width, axis=dim)
        before = lax.ppermute(last, axis, up)
        after = lax.ppermute(initial, axis, down)
        array = jnp.concatenate([before, array, after], axis=dim)
    return array


def laplace(padded, visc_pad):
    size_x = padded.shape[1] - 2
    size_y = padded.shape[2] - 2
    size_z = padded.shape[3] - 2
    centre = padded[:, 1 : 1 + size_x, 1 : 1 + size_y, 1 : 1 + size_z]
    visc_mid = visc_pad[1 : 1 + size_x, 1 : 1 + size_y, 1 : 1 + size_z]
    result = jnp.zeros_like(centre)
    for offset in ((2, 1, 1), (0, 1, 1), (1, 2, 1), (1, 0, 1), (1, 1, 2), (1, 1, 0)):
        first, second, third = offset
        beside = padded[:, first : first + size_x, second : second + size_y, third : third + size_z]
        visc_beside = visc_pad[
            first : first + size_x, second : second + size_y, third : third + size_z
        ]
        result = result + 0.5 * (visc_mid + visc_beside) * (beside - centre)
    return result


def factorize(panel, total_rows):
    local_gram = (
        lax.dot_general(
            panel,
            panel,
            (((1,), (1,)), ((), ())),
            precision=lax.Precision.HIGHEST,
            preferred_element_type=jnp.float32,
        )
        / total_rows
    )
    lower_factor = jnp.linalg.cholesky(lax.psum(local_gram, ("gx", "gy")))
    basis = jax.scipy.linalg.solve_triangular(lower_factor, panel, lower=True)
    return (lower_factor, basis)


def fields_rim_each(velocity, viscosity, forcing):
    visc_halo = padded_2(viscosity, (("gx", 0), ("gy", 1)), 1)
    visc_pad = jnp.pad(visc_halo, ((0, 0), (0, 0), (1, 1)))
    field = velocity
    fields = []
    for index in range(forcing.shape[0]):
        field_halo = padded_2(field, (("gx", 1), ("gy", 2)), 1)
        padded = jnp.pad(field_halo, ((0, 0), (0, 0), (0, 0), (1, 1)))
        field = field + laplace(padded, visc_pad) + forcing[index]
        fields.append(field)
    return fields


def local(velocity, viscosity, forcing, earlier):
    cell_rows = velocity.shape[0] * velocity.shape[1] * velocity.shape[2] * velocity.shape[3]
    total_rows = cell_rows * lax.axis_size("gx") * lax.axis_size("gy")
    fields = fields_rim_each(velocity, viscosity, forcing)
    panel_old = earlier.reshape(earlier.shape[0], cell_rows)
    snapshots = [field.reshape(1, cell_rows) for field in fields]
    lower_factor, basis = factorize(jnp.concatenate([panel_old] + snapshots, 0), total_rows)
    return (fields[-1], basis.reshape((basis.shape[0],) + velocity.shape), lower_factor.T)


def solution(mesh):
    return jax.shard_map(
        local,
        mesh=mesh,
        in_specs=(
            P(None, "gx", "gy", None),
            P("gx", "gy", None),
            P(None, None, "gx", "gy", None),
            P(None, None, "gx", "gy", None),
        ),
        out_specs=(P(None, "gx", "gy", None), P(None, None, "gx", "gy", None), P()),
        check_vma=False,
    )
```

profile of v0, /device:TPU:0, one launch (start us, length us, event | category | flops | bytes accessed | tf_op | source)
XLA Modules:
  0.0 195.6 jit_solution(2520877468651563737)
XLA Ops:
  0.6 0.9 fusion.91
  1.5 2.6 %collective-permute-start.2 = (f32[1,8,128]{2,1,0:T(8,128)S(1)}, f32[1,8,128]{2,1,0:T(8,128)S(1)}, u32[]{:S(2)}, u32[]{:S(2)}) collective-permute-start(f32[1,8,128]{2,1,0:T(8,128)S(1)} %get-tuple-element.39), channel_id=1, source_target_pairs={{0,8},{8,16},{16,24},{1,9},{9,17},{17,25},{2,10},{10,18},{18,26},{... | collective-permute-start | bytes 12296 | tf_op jit(solution)/shard_map/ppermute | solution.py:14
  4.1 1.3 collective-permute-start
  5.4 3.9 %collective-permute-done = f32[1,8,128]{2,1,0:T(8,128)S(1)} collective-permute-done((f32[1,8,128]{2,1,0:T(8,128)S(1)}, f32[1,8,128]{2,1,0:T(8,128)S(1)}, u32[]{:S(2)}, u32[]{:S(2)}) %collective-permute-start) | collective-permute-done | bytes 4128 | tf_op jit(solution)/shard_map/ppermute | solution.py:15
  9.3 0.9 fusion.81
  10.2 3.4 %collective-permute-start.6 = (f32[10,1,128]{2,1,0:T(1,128)S(1)}, f32[10,1,128]{2,1,0:T(1,128)S(1)}, u32[]{:S(2)}, u32[]{:S(2)}) collective-permute-start(f32[10,1,128]{2,1,0:T(1,128)S(1)} %get-tuple-element.29), channel_id=1, source_target_pairs={{0,1},{1,2},{2,3},{3,4},{4,5},{5,6},{6,7},{8,9},{9,10},{10,11},{11... | collective-permute-start | bytes 15368 | tf_op jit(solution)/shard_map/ppermute | solution.py:14
  13.6 1.3 collective-permute-start.4
  14.9 0.7 fusion.89
  15.6 1.3 collective-permute-start.1
  16.9 4.6 %collective-permute-start.3 = (f32[3,1,8,128]{3,2,1,0:T(8,128)S(1)}, f32[3,1,8,128]{3,2,1,0:T(8,128)S(1)}, u32[]{:S(2)}, u32[]{:S(2)}) collective-permute-start(f32[3,1,8,128]{3,2,1,0:T(8,128)S(1)} %get-tuple-element.26), channel_id=1, source_target_pairs={{0,8},{8,16},{16,24},{1,9},{9,17},{17,25},{2,10},{10,18},{18,26},{... | collective-permute-start | bytes 36872 | tf_op jit(solution)/shard_map/ppermute | solution.py:14
  21.6 0.0 collective-permute-done.6
  21.6 0.0 collective-permute-done.4
  21.6 0.1 select_maximum_fusion.14
  21.7 0.6 collective-permute-done.3
  22.4 0.9 constant_dynamic-update-slice_fusion.4
  23.3 0.0 collective-permute-done.1
  23.3 4.3 %collective-permute-start.7 = (f32[3,10,1,128]{3,2,1,0:T(1,128)S(1)}, f32[3,10,1,128]{3,2,1,0:T(1,128)S(1)}, u32[]{:S(2)}, u32[]{:S(2)}) collective-permute-start(f32[3,10,1,128]{3,2,1,0:T(1,128)S(1)} %get-tuple-element.17), channel_id=1, source_target_pairs={{0,1},{1,2},{2,3},{3,4},{4,5},{5,6},{6,7},{8,9},{9,10},{10,11},{11... | collective-permute-start | bytes 46088 | tf_op jit(solution)/shard_map/ppermute | solution.py:14
  27.6 1.3 collective-permute-start.5
  28.9 0.8 fusion.77
  29.7 0.0 collective-permute-done.7
  29.8 3.9 %collective-permute-done.5 = f32[3,10,1,128]{3,2,1,0:T(1,128)S(1)} collective-permute-done((f32[3,10,1,128]{3,2,1,0:T(1,128)S(1)}, f32[3,10,1,128]{3,2,1,0:T(1,128)S(1)}, u32[]{:S(2)}, u32[]{:S(2)}) %collective-permute-start.5) | collective-permute-done | bytes 15392 | tf_op jit(solution)/shard_map/ppermute | solution.py:15
  33.7 0.3 select_maximum_fusion.12
  34.0 1.2 fusion.58
  35.2 2.5 %collective-permute-start.9 = (f32[3,1,8,128]{3,2,1,0:T(8,128)S(1)}, f32[3,1,8,128]{3,2,1,0:T(8,128)S(1)}, u32[]{:S(2)}, u32[]{:S(2)}) collective-permute-start(f32[3,1,8,128]{3,2,1,0:T(8,128)S(1)} %get-tuple-element.23), channel_id=1, source_target_pairs={{0,8},{8,16},{16,24},{1,9},{9,17},{17,25},{2,10},{10,18},{18,26},{... | collective-permute-start | bytes 36872 | tf_op jit(solution)/shard_map/ppermute | solution.py:14
  37.7 1.3 collective-permute-start.8
  39.0 4.7 %collective-permute-done.8 = f32[3,1,8,128]{3,2,1,0:T(8,128)S(1)} collective-permute-done((f32[3,1,8,128]{3,2,1,0:T(8,128)S(1)}, f32[3,1,8,128]{3,2,1,0:T(8,128)S(1)}, u32[]{:S(2)}, u32[]{:S(2)}) %collective-permute-start.8) | collective-permute-done | bytes 12320 | tf_op jit(solution)/shard_map/ppermute | solution.py:15
  43.7 4.8 %collective-permute-start.11 = (f32[3,10,1,128]{3,2,1,0:T(1,128)S(1)}, f32[3,10,1,128]{3,2,1,0:T(1,128)S(1)}, u32[]{:S(2)}, u32[]{:S(2)}) collective-permute-start(f32[3,10,1,128]{3,2,1,0:T(1,128)S(1)} %get-tuple-element.15), channel_id=1, source_target_pairs={{0,1},{1,2},{2,3},{3,4},{4,5},{5,6},{6,7},{8,9},{9,10},{10,11},{11... | collective-permute-start | bytes 46088 | tf_op jit(solution)/shard_map/ppermute | solution.py:14
  48.6 1.3 collective-permute-start.10
  49.9 0.1 collective-permute-done.11
  50.0 4.2 %collective-permute-done.10 = f32[3,10,1,128]{3,2,1,0:T(1,128)S(1)} collective-permute-done((f32[3,10,1,128]{3,2,1,0:T(1,128)S(1)}, f32[3,10,1,128]{3,2,1,0:T(1,128)S(1)}, u32[]{:S(2)}, u32[]{:S(2)}) %collective-permute-start.10) | collective-permute-done | bytes 15392 | tf_op jit(solution)/shard_map/ppermute | solution.py:15
  54.2 0.3 select_maximum_fusion.8
  54.5 1.0 fusion.41
  55.6 2.9 %collective-permute-start.13 = (f32[3,1,8,128]{3,2,1,0:T(8,128)S(1)}, f32[3,1,8,128]{3,2,1,0:T(8,128)S(1)}, u32[]{:S(2)}, u32[]{:S(2)}) collective-permute-start(f32[3,1,8,128]{3,2,1,0:T(8,128)S(1)} %get-tuple-element.21), channel_id=1, source_target_pairs={{0,8},{8,16},{16,24},{1,9},{9,17},{17,25},{2,10},{10,18},{18,26},{... | collective-permute-start | bytes 36872 | tf_op jit(solution)/shard_map/ppermute | solution.py:14
  58.5 1.3 collective-permute-start.12
  59.8 2.7 %collective-permute-done.12 = f32[3,1,8,128]{3,2,1,0:T(8,128)S(1)} collective-permute-done((f32[3,1,8,128]{3,2,1,0:T(8,128)S(1)}, f32[3,1,8,128]{3,2,1,0:T(8,128)S(1)}, u32[]{:S(2)}, u32[]{:S(2)}) %collective-permute-start.12) | collective-permute-done | bytes 12320 | tf_op jit(solution)/shard_map/ppermute | solution.py:15
  62.5 2.9 %collective-permute-start.15 = (f32[3,10,1,128]{3,2,1,0:T(1,128)S(1)}, f32[3,10,1,128]{3,2,1,0:T(1,128)S(1)}, u32[]{:S(2)}, u32[]{:S(2)}) collective-permute-start(f32[3,10,1,128]{3,2,1,0:T(1,128)S(1)} %get-tuple-element.13), channel_id=1, source_target_pairs={{0,1},{1,2},{2,3},{3,4},{4,5},{5,6},{6,7},{8,9},{9,10},{10,11},{11... | collective-permute-start | bytes 46088 | tf_op jit(solution)/shard_map/ppermute | solution.py:14
  65.5 1.3 collective-permute-start.14
  66.8 0.1 collective-permute-done.15
  66.9 4.2 %collective-permute-done.14 = f32[3,10,1,128]{3,2,1,0:T(1,128)S(1)} collective-permute-done((f32[3,10,1,128]{3,2,1,0:T(1,128)S(1)}, f32[3,10,1,128]{3,2,1,0:T(1,128)S(1)}, u32[]{:S(2)}, u32[]{:S(2)}) %collective-permute-start.14) | collective-permute-done | bytes 15392 | tf_op jit(solution)/shard_map/ppermute | solution.py:15
  71.1 0.3 select_maximum_fusion.4
  71.5 1.0 fusion.24
  72.5 3.2 %collective-permute-start.17 = (f32[3,1,8,128]{3,2,1,0:T(8,128)S(1)}, f32[3,1,8,128]{3,2,1,0:T(8,128)S(1)}, u32[]{:S(2)}, u32[]{:S(2)}) collective-permute-start(f32[3,1,8,128]{3,2,1,0:T(8,128)S(1)} %get-tuple-element.19), channel_id=1, source_target_pairs={{0,8},{8,16},{16,24},{1,9},{9,17},{17,25},{2,10},{10,18},{18,26},{... | collective-permute-start | bytes 36872 | tf_op jit(solution)/shard_map/ppermute | solution.py:14
  75.7 1.3 collective-permute-start.16
  77.0 0.0 collective-permute-done.17
  77.0 2.4 %collective-permute-done.16 = f32[3,1,8,128]{3,2,1,0:T(8,128)S(1)} collective-permute-done((f32[3,1,8,128]{3,2,1,0:T(8,128)S(1)}, f32[3,1,8,128]{3,2,1,0:T(8,128)S(1)}, u32[]{:S(2)}, u32[]{:S(2)}) %collective-permute-start.16) | collective-permute-done | bytes 12320 | tf_op jit(solution)/shard_map/ppermute | solution.py:15
  79.5 4.8 %collective-permute-start.19 = (f32[3,10,1,128]{3,2,1,0:T(1,128)S(1)}, f32[3,10,1,128]{3,2,1,0:T(1,128)S(1)}, u32[]{:S(2)}, u32[]{:S(2)}) collective-permute-start(f32[3,10,1,128]{3,2,1,0:T(1,128)S(1)} %get-tuple-element.11), channel_id=1, source_target_pairs={{0,1},{1,2},{2,3},{3,4},{4,5},{5,6},{6,7},{8,9},{9,10},{10,11},{11... | collective-permute-start | bytes 46088 | tf_op jit(solution)/shard_map/ppermute | solution.py:14
  84.3 1.3 collective-permute-start.18
  85.6 1.0 pad.195
  86.6 6.3 %copy.21 = f32[8,8,192,128]{3,1,2,0:T(8,128)} copy(f32[8,8,192,128]{3,2,1,0:T(8,128)S(1)} %bitcast.40) | data formatting | bytes 12582912
  92.9 0.3 select_maximum_fusion
  93.2 1.0 fusion.7
  94.3 0.0 copy-start.1
  94.3 17.8 %concatenate.123 = f32[64,24576]{1,0:T(8,128)} concatenate(f32[60,24576]{1,0:T(8,128)} %bitcast.38, f32[1,24576]{1,0:T(1,128)S(1)} %bitcast.42, f32[1,24576]{1,0:T(1,128)S(1)} %bitcast.43, f32[1,24576]{1,0:T(1,128)S(1)} %bitcast.44, f32[1,24576]{1,0:T(1,128)S(1)} %bitcast.45), dimensions={0} | concatenate | bytes 12582912 | tf_op jit(solution)/shard_map/concatenate | solution.py:72
  112.1 8.2 %convolution_multiply_fusion = f32[64,64]{0,1:T(8,128)S(1)} fusion(f32[64,24576]{1,0:T(8,128)} %concatenate.123), kind=kOutput, calls=%fused_computation.2 | convolution fusion | flops 1207963648 | bytes 6307840 | tf_op jit(solution)/shard_map/dot_general | solution.py:39
  120.2 42.6 %psum.7 = f32[64,64]{0,1:T(8,128)S(1)} all-reduce(f32[64,64]{0,1:T(8,128)S(1)} %convolution_multiply_fusion), channel_id=1, replica_groups=mesh['gx'=4,'gy'=8] {'gx','gy'}, use_global_device_ids=true, to_apply=%region_0.1 | all-reduce | flops 4096 | bytes 32768 | tf_op jit(solution)/shard_map/psum | solution.py:48
  162.9 0.1 copy.13
  163.0 5.8 %cholesky.16 = f32[64,64]{1,0:T(8,128)S(1)} custom-call(f32[64,64]{1,0:T(8,128)S(1)} %fusion.83), custom_call_target="Cholesky" | custom-call | tf_op jit(solution)/shard_map/jit(cholesky)/cholesky | solution.py:48
  168.8 0.6 compare_reduce_fusion
  169.5 0.7 fusion.84
  170.1 0.7 copy.17
  170.8 4.9 %custom-call.7 = f32[1,64,64]{1,2,0:T(8,128)S(1)} custom-call(f32[1,64,64]{2,1,0:T(8,128)S(1)} %get-tuple-element.32), custom_call_target="InvertDiagBlocksLowerTriangular" | custom-call | tf_op jit(solution)/shard_map/jit(_solve_triangular)/triangular_solve | solution.py:49
  175.7 3.9 %copy.22 = f32[8,8,192,128]{3,2,1,0:T(8,128)S(1)} copy(f32[8,8,192,128]{3,1,2,0:T(8,128)} %bitcast.37) | data formatting | bytes 12582912
  179.7 9.3 %fusion = f32[64,3,8,8,128]{4,0,3,2,1:T(8,128)S(1)} fusion(f32[3,8,8,128,64]{3,2,1,0,4:T(8,128)S(1)} %bitcast.39, f32[1,64,64]{1,2,0:T(8,128)S(1)} %custom-call.7), kind=kOutput, calls=%fused_computation | convolution fusion | flops 1207959552 | bytes 12599296 | tf_op jit(solution)/shard_map/jit(_solve_triangular)/triangular_solve | solution.py:49
  189.0 6.6 %copy.16 = f32[64,3,8,8,128]{4,3,2,1,0:T(8,128)} copy(f32[64,3,8,8,128]{4,0,3,2,1:T(8,128)S(1)} %fusion) | data formatting | bytes 12582912
  (22 shorter events, 0.2 us)
Async XLA Ops:
  0.6 85.0 %copy-start = (f32[60,3,8,8,128]{4,3,2,1,0:T(8,128)S(1)}, f32[60,3,8,8,128]{4,3,2,1,0:T(8,128)}, u32[]{:S(2)}) copy-start(f32[60,3,8,8,128]{4,3,2,1,0:T(8,128)} %param.7) | copy-start | bytes 17694724
  1.5 3.9 %collective-permute-start.2 = (f32[1,8,128]{2,1,0:T(8,128)S(1)}, f32[1,8,128]{2,1,0:T(8,128)S(1)}, u32[]{:S(2)}, u32[]{:S(2)}) collective-permute-start(f32[1,8,128]{2,1,0:T(8,128)S(1)} %get-tuple-element.39), channel_id=1, source_target_pairs={{0,8},{8,16},{16,24},{1,9},{9,17},{17,25},{2,10},{10,18},{18,26},{... | collective-permute-start | bytes 12296 | tf_op jit(solution)/shard_map/ppermute | solution.py:14
  4.1 5.2 %collective-permute-start = (f32[1,8,128]{2,1,0:T(8,128)S(1)}, f32[1,8,128]{2,1,0:T(8,128)S(1)}, u32[]{:S(2)}, u32[]{:S(2)}) collective-permute-start(f32[1,8,128]{2,1,0:T(8,128)S(1)} %get-tuple-element.38), channel_id=1, source_target_pairs={{8,0},{16,8},{24,16},{9,1},{17,9},{25,17},{10,2},{18,10},{26,18},{... | collective-permute-start | bytes 12296 | tf_op jit(solution)/shard_map/ppermute | solution.py:15
  10.2 11.3 %collective-permute-start.6 = (f32[10,1,128]{2,1,0:T(1,128)S(1)}, f32[10,1,128]{2,1,0:T(1,128)S(1)}, u32[]{:S(2)}, u32[]{:S(2)}) collective-permute-start(f32[10,1,128]{2,1,0:T(1,128)S(1)} %get-tuple-element.29), channel_id=1, source_target_pairs={{0,1},{1,2},{2,3},{3,4},{4,5},{5,6},{6,7},{8,9},{9,10},{10,11},{11... | collective-permute-start | bytes 15368 | tf_op jit(solution)/shard_map/ppermute | solution.py:14
  13.6 8.0 %collective-permute-start.4 = (f32[10,1,128]{2,1,0:T(1,128)S(1)}, f32[10,1,128]{2,1,0:T(1,128)S(1)}, u32[]{:S(2)}, u32[]{:S(2)}) collective-permute-start(f32[10,1,128]{2,1,0:T(1,128)S(1)} %get-tuple-element.30), channel_id=1, source_target_pairs={{1,0},{2,1},{3,2},{4,3},{5,4},{6,5},{7,6},{9,8},{10,9},{11,10},{12... | collective-permute-start | bytes 15368 | tf_op jit(solution)/shard_map/ppermute | solution.py:15
  15.6 7.6 %collective-permute-start.1 = (f32[3,1,8,128]{3,2,1,0:T(8,128)S(1)}, f32[3,1,8,128]{3,2,1,0:T(8,128)S(1)}, u32[]{:S(2)}, u32[]{:S(2)}) collective-permute-start(f32[3,1,8,128]{3,2,1,0:T(8,128)S(1)} %get-tuple-element.25), channel_id=1, source_target_pairs={{8,0},{16,8},{24,16},{9,1},{17,9},{25,17},{10,2},{18,10},{26,18},{... | collective-permute-start | bytes 36872 | tf_op jit(solution)/shard_map/ppermute | solution.py:15
  16.9 5.4 %collective-permute-start.3 = (f32[3,1,8,128]{3,2,1,0:T(8,128)S(1)}, f32[3,1,8,128]{3,2,1,0:T(8,128)S(1)}, u32[]{:S(2)}, u32[]{:S(2)}) collective-permute-start(f32[3,1,8,128]{3,2,1,0:T(8,128)S(1)} %get-tuple-element.26), channel_id=1, source_target_pairs={{0,8},{8,16},{16,24},{1,9},{9,17},{17,25},{2,10},{10,18},{18,26},{... | collective-permute-start | bytes 36872 | tf_op jit(solution)/shard_map/ppermute | solution.py:14
  23.3 6.4 %collective-permute-start.7 = (f32[3,10,1,128]{3,2,1,0:T(1,128)S(1)}, f32[3,10,1,128]{3,2,1,0:T(1,128)S(1)}, u32[]{:S(2)}, u32[]{:S(2)}) collective-permute-start(f32[3,10,1,128]{3,2,1,0:T(1,128)S(1)} %get-tuple-element.17), channel_id=1, source_target_pairs={{0,1},{1,2},{2,3},{3,4},{4,5},{5,6},{6,7},{8,9},{9,10},{10,11},{11... | collective-permute-start | bytes 46088 | tf_op jit(solution)/shard_map/ppermute | solution.py:14
  27.6 6.1 %collective-permute-start.5 = (f32[3,10,1,128]{3,2,1,0:T(1,128)S(1)}, f32[3,10,1,128]{3,2,1,0:T(1,128)S(1)}, u32[]{:S(2)}, u32[]{:S(2)}) collective-permute-start(f32[3,10,1,128]{3,2,1,0:T(1,128)S(1)} %get-tuple-element.18), channel_id=1, source_target_pairs={{1,0},{2,1},{3,2},{4,3},{5,4},{6,5},{7,6},{9,8},{10,9},{11,10},{12... | collective-permute-start | bytes 46088 | tf_op jit(solution)/shard_map/ppermute | solution.py:15
  35.2 3.8 %collective-permute-start.9 = (f32[3,1,8,128]{3,2,1,0:T(8,128)S(1)}, f32[3,1,8,128]{3,2,1,0:T(8,128)S(1)}, u32[]{:S(2)}, u32[]{:S(2)}) collective-permute-start(f32[3,1,8,128]{3,2,1,0:T(8,128)S(1)} %get-tuple-element.23), channel_id=1, source_target_pairs={{0,8},{8,16},{16,24},{1,9},{9,17},{17,25},{2,10},{10,18},{18,26},{... | collective-permute-start | bytes 36872 | tf_op jit(solution)/shard_map/ppermute | solution.py:14
  37.7 6.0 %collective-permute-start.8 = (f32[3,1,8,128]{3,2,1,0:T(8,128)S(1)}, f32[3,1,8,128]{3,2,1,0:T(8,128)S(1)}, u32[]{:S(2)}, u32[]{:S(2)}) collective-permute-start(f32[3,1,8,128]{3,2,1,0:T(8,128)S(1)} %get-tuple-element.24), channel_id=1, source_target_pairs={{8,0},{16,8},{24,16},{9,1},{17,9},{25,17},{10,2},{18,10},{26,18},{... | collective-permute-start | bytes 36872 | tf_op jit(solution)/shard_map/ppermute | solution.py:15
  43.7 6.2 %collective-permute-start.11 = (f32[3,10,1,128]{3,2,1,0:T(1,128)S(1)}, f32[3,10,1,128]{3,2,1,0:T(1,128)S(1)}, u32[]{:S(2)}, u32[]{:S(2)}) collective-permute-start(f32[3,10,1,128]{3,2,1,0:T(1,128)S(1)} %get-tuple-element.15), channel_id=1, source_target_pairs={{0,1},{1,2},{2,3},{3,4},{4,5},{5,6},{6,7},{8,9},{9,10},{10,11},{11... | collective-permute-start | bytes 46088 | tf_op jit(solution)/shard_map/ppermute | solution.py:14
  48.6 5.6 %collective-permute-start.10 = (f32[3,10,1,128]{3,2,1,0:T(1,128)S(1)}, f32[3,10,1,128]{3,2,1,0:T(1,128)S(1)}, u32[]{:S(2)}, u32[]{:S(2)}) collective-permute-start(f32[3,10,1,128]{3,2,1,0:T(1,128)S(1)} %get-tuple-element.16), channel_id=1, source_target_pairs={{1,0},{2,1},{3,2},{4,3},{5,4},{6,5},{7,6},{9,8},{10,9},{11,10},{12... | collective-permute-start | bytes 46088 | tf_op jit(solution)/shard_map/ppermute | solution.py:15
  55.6 4.2 %collective-permute-start.13 = (f32[3,1,8,128]{3,2,1,0:T(8,128)S(1)}, f32[3,1,8,128]{3,2,1,0:T(8,128)S(1)}, u32[]{:S(2)}, u32[]{:S(2)}) collective-permute-start(f32[3,1,8,128]{3,2,1,0:T(8,128)S(1)} %get-tuple-element.21), channel_id=1, source_target_pairs={{0,8},{8,16},{16,24},{1,9},{9,17},{17,25},{2,10},{10,18},{18,26},{... | collective-permute-start | bytes 36872 | tf_op jit(solution)/shard_map/ppermute | solution.py:14
  58.5 4.0 %collective-permute-start.12 = (f32[3,1,8,128]{3,2,1,0:T(8,128)S(1)}, f32[3,1,8,128]{3,2,1,0:T(8,128)S(1)}, u32[]{:S(2)}, u32[]{:S(2)}) collective-permute-start(f32[3,1,8,128]{3,2,1,0:T(8,128)S(1)} %get-tuple-element.22), channel_id=1, source_target_pairs={{8,0},{16,8},{24,16},{9,1},{17,9},{25,17},{10,2},{18,10},{26,18},{... | collective-permute-start | bytes 36872 | tf_op jit(solution)/shard_map/ppermute | solution.py:15
  62.5 4.4 %collective-permute-start.15 = (f32[3,10,1,128]{3,2,1,0:T(1,128)S(1)}, f32[3,10,1,128]{3,2,1,0:T(1,128)S(1)}, u32[]{:S(2)}, u32[]{:S(2)}) collective-permute-start(f32[3,10,1,128]{3,2,1,0:T(1,128)S(1)} %get-tuple-element.13), channel_id=1, source_target_pairs={{0,1},{1,2},{2,3},{3,4},{4,5},{5,6},{6,7},{8,9},{9,10},{10,11},{11... | collective-permute-start | bytes 46088 | tf_op jit(solution)/shard_map/ppermute | solution.py:14
  65.5 5.6 %collective-permute-start.14 = (f32[3,10,1,128]{3,2,1,0:T(1,128)S(1)}, f32[3,10,1,128]{3,2,1,0:T(1,128)S(1)}, u32[]{:S(2)}, u32[]{:S(2)}) collective-permute-start(f32[3,10,1,128]{3,2,1,0:T(1,128)S(1)} %get-tuple-element.14), channel_id=1, source_target_pairs={{1,0},{2,1},{3,2},{4,3},{5,4},{6,5},{7,6},{9,8},{10,9},{11,10},{12... | collective-permute-start | bytes 46088 | tf_op jit(solution)/shard_map/ppermute | solution.py:15
  72.5 4.5 %collective-permute-start.17 = (f32[3,1,8,128]{3,2,1,0:T(8,128)S(1)}, f32[3,1,8,128]{3,2,1,0:T(8,128)S(1)}, u32[]{:S(2)}, u32[]{:S(2)}) collective-permute-start(f32[3,1,8,128]{3,2,1,0:T(8,128)S(1)} %get-tuple-element.19), channel_id=1, source_target_pairs={{0,8},{8,16},{16,24},{1,9},{9,17},{17,25},{2,10},{10,18},{18,26},{... | collective-permute-start | bytes 36872 | tf_op jit(solution)/shard_map/ppermute | solution.py:14
  75.7 3.8 %collective-permute-start.16 = (f32[3,1,8,128]{3,2,1,0:T(8,128)S(1)}, f32[3,1,8,128]{3,2,1,0:T(8,128)S(1)}, u32[]{:S(2)}, u32[]{:S(2)}) collective-permute-start(f32[3,1,8,128]{3,2,1,0:T(8,128)S(1)} %get-tuple-element.20), channel_id=1, source_target_pairs={{8,0},{16,8},{24,16},{9,1},{17,9},{25,17},{10,2},{18,10},{26,18},{... | collective-permute-start | bytes 36872 | tf_op jit(solution)/shard_map/ppermute | solution.py:15
  79.5 13.4 %collective-permute-start.19 = (f32[3,10,1,128]{3,2,1,0:T(1,128)S(1)}, f32[3,10,1,128]{3,2,1,0:T(1,128)S(1)}, u32[]{:S(2)}, u32[]{:S(2)}) collective-permute-start(f32[3,10,1,128]{3,2,1,0:T(1,128)S(1)} %get-tuple-element.11), channel_id=1, source_target_pairs={{0,1},{1,2},{2,3},{3,4},{4,5},{5,6},{6,7},{8,9},{9,10},{10,11},{11... | collective-permute-start | bytes 46088 | tf_op jit(solution)/shard_map/ppermute | solution.py:14
  84.3 8.6 %collective-permute-start.18 = (f32[3,10,1,128]{3,2,1,0:T(1,128)S(1)}, f32[3,10,1,128]{3,2,1,0:T(1,128)S(1)}, u32[]{:S(2)}, u32[]{:S(2)}) collective-permute-start(f32[3,10,1,128]{3,2,1,0:T(1,128)S(1)} %get-tuple-element.12), channel_id=1, source_target_pairs={{1,0},{2,1},{3,2},{4,3},{5,4},{6,5},{7,6},{9,8},{10,9},{11,10},{12... | collective-permute-start | bytes 46088 | tf_op jit(solution)/shard_map/ppermute | solution.py:15
  94.3 17.8 %copy-start.1 = (f32[3,8,8,128]{3,2,1,0:T(8,128)}, f32[3,8,8,128]{3,2,1,0:T(8,128)S(1)}, u32[]{:S(2)}) copy-start(f32[3,8,8,128]{3,2,1,0:T(8,128)S(1)} %fusion.7) | copy-start | bytes 294916
where the time goes:
time: 197 us; the launch traced here: 196 us
  starting transfers between devices  49 us (25%)
  blocking collectives  42.6 us (22%)
  local copies, waits for them, and re-layouts  38.9 us (20%)
  waiting for transfers between devices  27 us (14%)
  other arithmetic  19.6 us (10%)
  matrix products  17.5 us (9%)
    psum x1, blocking collectives, factorize(): lower_factor = jnp.linalg.cholesky(lax.psum(local_gram, ('gx', 'gy')))  42.6 us
    ppermute x10, starting transfers between devices, padded_2(): before = lax.ppermute(last, axis, up)  36.1 us
    ppermute x10, waiting for transfers between devices, padded_2(): after = lax.ppermute(initial, axis, down)  26.1 us
    unnamed x12, local copies, waits for them, and re-layouts  19.4 us
    concatenate x1, local copies, waits for them, and re-layouts, local(): jnp.concatenate([panel_old] + snapshots, 0)  17.8 us
    ppermute x10, starting transfers between devices, padded_2(): after = lax.ppermute(initial, axis, down)  12.9 us
    another operation x1, matrix products, factorize(): basis = jax.scipy.linalg.solve_triangular(lower_factor, panel, lower=True)  9.33 us
    dot_general x1, matrix products, factorize(): lax.dot_general(panel, panel, (((1,), (1,)), ((), ())), precision=lax.Pre...  8.18 us
  transfers between devices with their start and end apart: 20, of which 10 were waited for; matrix products, arithmetic and copies ran while one was open for 5% of the time, Pallas kernels for 0%

commit v1 on v0

--- a/solution.py
+++ b/solution.py
@@ -45,7 +45,10 @@
         )
         / total_rows
     )
-    lower_factor = jnp.linalg.cholesky(lax.psum(local_gram, ("gx", "gy")))
+    attach_panel = lambda array_here, mesh_ax, along_axis: lax.psum(
+        lax.psum(array_here, mesh_ax), along_axis
+    )
+    lower_factor = jnp.linalg.cholesky(attach_panel(local_gram, "gx", "gy"))
     basis = jax.scipy.linalg.solve_triangular(lower_factor, panel, lower=True)
     return (lower_factor, basis)
 

time: 197 us -> 202 us (1.025)
  blocking collectives: 42.6 us -> 47.7 us
    psum x1 -> x2, blocking collectives: 42.6 us -> 47.7 us  [the longest x1 35.4 us: factorize(): lax.psum(lax.psum(array_here, mesh_ax), along_axis)]
where the time goes in v1:
time: 202 us; the launch traced here: 201 us
  starting transfers between devices  49 us (24%)
  blocking collectives  47.7 us (24%)
  local copies, waits for them, and re-layouts  38.8 us (19%)
  waiting for transfers between devices  27 us (13%)
  other arithmetic  19.6 us (10%)
  matrix products  17.5 us (9%)
    ppermute x10, starting transfers between devices, padded_2(): before = lax.ppermute(last, axis, up)  36.1 us
    psum x1, blocking collectives, factorize(): lax.psum(lax.psum(array_here, mesh_ax), along_axis)  35.4 us
    ppermute x10, waiting for transfers between devices, padded_2(): after = lax.ppermute(initial, axis, down)  26.1 us
    unnamed x12, local copies, waits for them, and re-layouts  19.4 us
    concatenate x1, local copies, waits for them, and re-layouts, local(): jnp.concatenate([panel_old] + snapshots, 0)  17.7 us
    ppermute x10, starting transfers between devices, padded_2(): after = lax.ppermute(initial, axis, down)  12.9 us
    psum x1, blocking collectives, factorize(): lax.psum(array_here, mesh_ax)  12.3 us
    another operation x1, matrix products, factorize(): basis = jax.scipy.linalg.solve_triangular(lower_factor, panel, lower=True)  9.33 us
  transfers between devices with their start and end apart: 20, of which 10 were waited for; matrix products, arithmetic and copies ran while one was open for 5% of the time, Pallas kernels for 0%

profile of v1, /device:TPU:0, one launch (start us, length us, event | category | flops | bytes accessed | tf_op | source)
XLA Modules:
  0.0 200.6 jit_solution(14532236857107992846)
XLA Ops:
  0.6 0.9 fusion.91
  1.5 2.6 %collective-permute-start.2 = (f32[1,8,128]{2,1,0:T(8,128)S(1)}, f32[1,8,128]{2,1,0:T(8,128)S(1)}, u32[]{:S(2)}, u32[]{:S(2)}) collective-permute-start(f32[1,8,128]{2,1,0:T(8,128)S(1)} %get-tuple-element.39), channel_id=1, source_target_pairs={{0,8},{8,16},{16,24},{1,9},{9,17},{17,25},{2,10},{10,18},{18,26},{... | collective-permute-start | bytes 12296 | tf_op jit(solution)/shard_map/ppermute | solution.py:14
  4.1 1.3 collective-permute-start
  5.4 3.9 %collective-permute-done = f32[1,8,128]{2,1,0:T(8,128)S(1)} collective-permute-done((f32[1,8,128]{2,1,0:T(8,128)S(1)}, f32[1,8,128]{2,1,0:T(8,128)S(1)}, u32[]{:S(2)}, u32[]{:S(2)}) %collective-permute-start) | collective-permute-done | bytes 4128 | tf_op jit(solution)/shard_map/ppermute | solution.py:15
  9.3 0.9 fusion.81
  10.2 3.4 %collective-permute-start.6 = (f32[10,1,128]{2,1,0:T(1,128)S(1)}, f32[10,1,128]{2,1,0:T(1,128)S(1)}, u32[]{:S(2)}, u32[]{:S(2)}) collective-permute-start(f32[10,1,128]{2,1,0:T(1,128)S(1)} %get-tuple-element.29), channel_id=1, source_target_pairs={{0,1},{1,2},{2,3},{3,4},{4,5},{5,6},{6,7},{8,9},{9,10},{10,11},{11... | collective-permute-start | bytes 15368 | tf_op jit(solution)/shard_map/ppermute | solution.py:14
  13.6 1.3 collective-permute-start.4
  14.9 0.7 fusion.89
  15.6 1.3 collective-permute-start.1
  16.9 4.6 %collective-permute-start.3 = (f32[3,1,8,128]{3,2,1,0:T(8,128)S(1)}, f32[3,1,8,128]{3,2,1,0:T(8,128)S(1)}, u32[]{:S(2)}, u32[]{:S(2)}) collective-permute-start(f32[3,1,8,128]{3,2,1,0:T(8,128)S(1)} %get-tuple-element.26), channel_id=1, source_target_pairs={{0,8},{8,16},{16,24},{1,9},{9,17},{17,25},{2,10},{10,18},{18,26},{... | collective-permute-start | bytes 36872 | tf_op jit(solution)/shard_map/ppermute | solution.py:14
  21.6 0.0 collective-permute-done.6
  21.6 0.0 collective-permute-done.4
  21.6 0.1 select_maximum_fusion.14
  21.7 0.6 collective-permute-done.3
  22.4 0.9 constant_dynamic-update-slice_fusion.4
  23.3 0.0 collective-permute-done.1
  23.3 4.3 %collective-permute-start.7 = (f32[3,10,1,128]{3,2,1,0:T(1,128)S(1)}, f32[3,10,1,128]{3,2,1,0:T(1,128)S(1)}, u32[]{:S(2)}, u32[]{:S(2)}) collective-permute-start(f32[3,10,1,128]{3,2,1,0:T(1,128)S(1)} %get-tuple-element.17), channel_id=1, source_target_pairs={{0,1},{1,2},{2,3},{3,4},{4,5},{5,6},{6,7},{8,9},{9,10},{10,11},{11... | collective-permute-start | bytes 46088 | tf_op jit(solution)/shard_map/ppermute | solution.py:14
  27.6 1.3 collective-permute-start.5
  28.9 0.8 fusion.77
  29.7 0.0 collective-permute-done.7
  29.8 3.9 %collective-permute-done.5 = f32[3,10,1,128]{3,2,1,0:T(1,128)S(1)} collective-permute-done((f32[3,10,1,128]{3,2,1,0:T(1,128)S(1)}, f32[3,10,1,128]{3,2,1,0:T(1,128)S(1)}, u32[]{:S(2)}, u32[]{:S(2)}) %collective-permute-start.5) | collective-permute-done | bytes 15392 | tf_op jit(solution)/shard_map/ppermute | solution.py:15
  33.7 0.3 select_maximum_fusion.12
  34.0 1.2 fusion.58
  35.2 2.5 %collective-permute-start.9 = (f32[3,1,8,128]{3,2,1,0:T(8,128)S(1)}, f32[3,1,8,128]{3,2,1,0:T(8,128)S(1)}, u32[]{:S(2)}, u32[]{:S(2)}) collective-permute-start(f32[3,1,8,128]{3,2,1,0:T(8,128)S(1)} %get-tuple-element.23), channel_id=1, source_target_pairs={{0,8},{8,16},{16,24},{1,9},{9,17},{17,25},{2,10},{10,18},{18,26},{... | collective-permute-start | bytes 36872 | tf_op jit(solution)/shard_map/ppermute | solution.py:14
  37.7 1.3 collective-permute-start.8
  39.0 4.7 %collective-permute-done.8 = f32[3,1,8,128]{3,2,1,0:T(8,128)S(1)} collective-permute-done((f32[3,1,8,128]{3,2,1,0:T(8,128)S(1)}, f32[3,1,8,128]{3,2,1,0:T(8,128)S(1)}, u32[]{:S(2)}, u32[]{:S(2)}) %collective-permute-start.8) | collective-permute-done | bytes 12320 | tf_op jit(solution)/shard_map/ppermute | solution.py:15
  43.7 4.8 %collective-permute-start.11 = (f32[3,10,1,128]{3,2,1,0:T(1,128)S(1)}, f32[3,10,1,128]{3,2,1,0:T(1,128)S(1)}, u32[]{:S(2)}, u32[]{:S(2)}) collective-permute-start(f32[3,10,1,128]{3,2,1,0:T(1,128)S(1)} %get-tuple-element.15), channel_id=1, source_target_pairs={{0,1},{1,2},{2,3},{3,4},{4,5},{5,6},{6,7},{8,9},{9,10},{10,11},{11... | collective-permute-start | bytes 46088 | tf_op jit(solution)/shard_map/ppermute | solution.py:14
  48.6 1.3 collective-permute-start.10
  49.9 0.1 collective-permute-done.11
  50.0 4.2 %collective-permute-done.10 = f32[3,10,1,128]{3,2,1,0:T(1,128)S(1)} collective-permute-done((f32[3,10,1,128]{3,2,1,0:T(1,128)S(1)}, f32[3,10,1,128]{3,2,1,0:T(1,128)S(1)}, u32[]{:S(2)}, u32[]{:S(2)}) %collective-permute-start.10) | collective-permute-done | bytes 15392 | tf_op jit(solution)/shard_map/ppermute | solution.py:15
  54.2 0.3 select_maximum_fusion.8
  54.5 1.0 fusion.41
  55.6 2.9 %collective-permute-start.13 = (f32[3,1,8,128]{3,2,1,0:T(8,128)S(1)}, f32[3,1,8,128]{3,2,1,0:T(8,128)S(1)}, u32[]{:S(2)}, u32[]{:S(2)}) collective-permute-start(f32[3,1,8,128]{3,2,1,0:T(8,128)S(1)} %get-tuple-element.21), channel_id=1, source_target_pairs={{0,8},{8,16},{16,24},{1,9},{9,17},{17,25},{2,10},{10,18},{18,26},{... | collective-permute-start | bytes 36872 | tf_op jit(solution)/shard_map/ppermute | solution.py:14
  58.5 1.3 collective-permute-start.12
  59.8 2.7 %collective-permute-done.12 = f32[3,1,8,128]{3,2,1,0:T(8,128)S(1)} collective-permute-done((f32[3,1,8,128]{3,2,1,0:T(8,128)S(1)}, f32[3,1,8,128]{3,2,1,0:T(8,128)S(1)}, u32[]{:S(2)}, u32[]{:S(2)}) %collective-permute-start.12) | collective-permute-done | bytes 12320 | tf_op jit(solution)/shard_map/ppermute | solution.py:15
  62.5 2.9 %collective-permute-start.15 = (f32[3,10,1,128]{3,2,1,0:T(1,128)S(1)}, f32[3,10,1,128]{3,2,1,0:T(1,128)S(1)}, u32[]{:S(2)}, u32[]{:S(2)}) collective-permute-start(f32[3,10,1,128]{3,2,1,0:T(1,128)S(1)} %get-tuple-element.13), channel_id=1, source_target_pairs={{0,1},{1,2},{2,3},{3,4},{4,5},{5,6},{6,7},{8,9},{9,10},{10,11},{11... | collective-permute-start | bytes 46088 | tf_op jit(solution)/shard_map/ppermute | solution.py:14
  65.5 1.3 collective-permute-start.14
  66.8 0.1 collective-permute-done.15
  66.9 4.2 %collective-permute-done.14 = f32[3,10,1,128]{3,2,1,0:T(1,128)S(1)} collective-permute-done((f32[3,10,1,128]{3,2,1,0:T(1,128)S(1)}, f32[3,10,1,128]{3,2,1,0:T(1,128)S(1)}, u32[]{:S(2)}, u32[]{:S(2)}) %collective-permute-start.14) | collective-permute-done | bytes 15392 | tf_op jit(solution)/shard_map/ppermute | solution.py:15
  71.1 0.3 select_maximum_fusion.4
  71.5 1.0 fusion.24
  72.5 3.2 %collective-permute-start.17 = (f32[3,1,8,128]{3,2,1,0:T(8,128)S(1)}, f32[3,1,8,128]{3,2,1,0:T(8,128)S(1)}, u32[]{:S(2)}, u32[]{:S(2)}) collective-permute-start(f32[3,1,8,128]{3,2,1,0:T(8,128)S(1)} %get-tuple-element.19), channel_id=1, source_target_pairs={{0,8},{8,16},{16,24},{1,9},{9,17},{17,25},{2,10},{10,18},{18,26},{... | collective-permute-start | bytes 36872 | tf_op jit(solution)/shard_map/ppermute | solution.py:14
  75.7 1.3 collective-permute-start.16
  77.0 2.4 %collective-permute-done.16 = f32[3,1,8,128]{3,2,1,0:T(8,128)S(1)} collective-permute-done((f32[3,1,8,128]{3,2,1,0:T(8,128)S(1)}, f32[3,1,8,128]{3,2,1,0:T(8,128)S(1)}, u32[]{:S(2)}, u32[]{:S(2)}) %collective-permute-start.16) | collective-permute-done | bytes 12320 | tf_op jit(solution)/shard_map/ppermute | solution.py:15
  79.5 4.8 %collective-permute-start.19 = (f32[3,10,1,128]{3,2,1,0:T(1,128)S(1)}, f32[3,10,1,128]{3,2,1,0:T(1,128)S(1)}, u32[]{:S(2)}, u32[]{:S(2)}) collective-permute-start(f32[3,10,1,128]{3,2,1,0:T(1,128)S(1)} %get-tuple-element.11), channel_id=1, source_target_pairs={{0,1},{1,2},{2,3},{3,4},{4,5},{5,6},{6,7},{8,9},{9,10},{10,11},{11... | collective-permute-start | bytes 46088 | tf_op jit(solution)/shard_map/ppermute | solution.py:14
  84.3 1.3 collective-permute-start.18
  85.6 1.0 pad.195
  86.6 6.3 %copy.21 = f32[8,8,192,128]{3,1,2,0:T(8,128)} copy(f32[8,8,192,128]{3,2,1,0:T(8,128)S(1)} %bitcast.40) | data formatting | bytes 12582912
  92.9 0.3 select_maximum_fusion
  93.2 1.0 fusion.7
  94.3 0.0 copy-start.1
  94.3 17.7 %concatenate.123 = f32[64,24576]{1,0:T(8,128)} concatenate(f32[60,24576]{1,0:T(8,128)} %bitcast.38, f32[1,24576]{1,0:T(1,128)S(1)} %bitcast.42, f32[1,24576]{1,0:T(1,128)S(1)} %bitcast.43, f32[1,24576]{1,0:T(1,128)S(1)} %bitcast.44, f32[1,24576]{1,0:T(1,128)S(1)} %bitcast.45), dimensions={0} | concatenate | bytes 12582912 | tf_op jit(solution)/shard_map/concatenate | solution.py:75
  112.0 8.2 %convolution_multiply_fusion = f32[64,64]{0,1:T(8,128)S(1)} fusion(f32[64,24576]{1,0:T(8,128)} %concatenate.123), kind=kOutput, calls=%fused_computation.2 | convolution fusion | flops 1207963648 | bytes 6307840 | tf_op jit(solution)/shard_map/dot_general | solution.py:39
  120.2 12.3 %psum.14 = f32[64,64]{0,1:T(8,128)S(1)} all-reduce(f32[64,64]{0,1:T(8,128)S(1)} %convolution_multiply_fusion), channel_id=1, replica_groups=mesh['gx'=4,'gy'=8] {'gx'}, use_global_device_ids=true, to_apply=%region_0.1 | all-reduce | flops 4096 | bytes 32768 | tf_op jit(solution)/shard_map/psum | solution.py:49
  132.5 35.4 %psum.15 = f32[64,64]{0,1:T(8,128)S(1)} all-reduce(f32[64,64]{0,1:T(8,128)S(1)} %psum.14), channel_id=1, replica_groups=mesh['gx'=4,'gy'=8] {'gy'}, use_global_device_ids=true, to_apply=%region_1.2 | all-reduce | flops 4096 | bytes 32768 | tf_op jit(solution)/shard_map/psum | solution.py:48
  167.9 0.1 copy.13
  168.0 5.8 %cholesky.16 = f32[64,64]{1,0:T(8,128)S(1)} custom-call(f32[64,64]{1,0:T(8,128)S(1)} %fusion.83), custom_call_target="Cholesky" | custom-call | tf_op jit(solution)/shard_map/jit(cholesky)/cholesky | solution.py:51
  173.9 0.6 compare_reduce_fusion
  174.5 0.7 fusion.84
  175.2 0.7 copy.17
  175.9 4.9 %custom-call.7 = f32[1,64,64]{1,2,0:T(8,128)S(1)} custom-call(f32[1,64,64]{2,1,0:T(8,128)S(1)} %get-tuple-element.32), custom_call_target="InvertDiagBlocksLowerTriangular" | custom-call | tf_op jit(solution)/shard_map/jit(_solve_triangular)/triangular_solve | solution.py:52
  180.8 3.9 %copy.22 = f32[8,8,192,128]{3,2,1,0:T(8,128)S(1)} copy(f32[8,8,192,128]{3,1,2,0:T(8,128)} %bitcast.37) | data formatting | bytes 12582912
  184.7 9.3 %fusion = f32[64,3,8,8,128]{4,0,3,2,1:T(8,128)S(1)} fusion(f32[3,8,8,128,64]{3,2,1,0,4:T(8,128)S(1)} %bitcast.39, f32[1,64,64]{1,2,0:T(8,128)S(1)} %custom-call.7), kind=kOutput, calls=%fused_computation | convolution fusion | flops 1207959552 | bytes 12599296 | tf_op jit(solution)/shard_map/jit(_solve_triangular)/triangular_solve | solution.py:52
  194.1 6.6 %copy.16 = f32[64,3,8,8,128]{4,3,2,1,0:T(8,128)} copy(f32[64,3,8,8,128]{4,0,3,2,1:T(8,128)S(1)} %fusion) | data formatting | bytes 12582912
  (23 shorter events, 0.2 us)
Async XLA Ops:
  0.6 85.0 %copy-start = (f32[60,3,8,8,128]{4,3,2,1,0:T(8,128)S(1)}, f32[60,3,8,8,128]{4,3,2,1,0:T(8,128)}, u32[]{:S(2)}) copy-start(f32[60,3,8,8,128]{4,3,2,1,0:T(8,128)} %param.7) | copy-start | bytes 17694724
  1.5 3.9 %collective-permute-start.2 = (f32[1,8,128]{2,1,0:T(8,128)S(1)}, f32[1,8,128]{2,1,0:T(8,128)S(1)}, u32[]{:S(2)}, u32[]{:S(2)}) collective-permute-start(f32[1,8,128]{2,1,0:T(8,128)S(1)} %get-tuple-element.39), channel_id=1, source_target_pairs={{0,8},{8,16},{16,24},{1,9},{9,17},{17,25},{2,10},{10,18},{18,26},{... | collective-permute-start | bytes 12296 | tf_op jit(solution)/shard_map/ppermute | solution.py:14
  4.1 5.2 %collective-permute-start = (f32[1,8,128]{2,1,0:T(8,128)S(1)}, f32[1,8,128]{2,1,0:T(8,128)S(1)}, u32[]{:S(2)}, u32[]{:S(2)}) collective-permute-start(f32[1,8,128]{2,1,0:T(8,128)S(1)} %get-tuple-element.38), channel_id=1, source_target_pairs={{8,0},{16,8},{24,16},{9,1},{17,9},{25,17},{10,2},{18,10},{26,18},{... | collective-permute-start | bytes 12296 | tf_op jit(solution)/shard_map/ppermute | solution.py:15
  10.2 11.3 %collective-permute-start.6 = (f32[10,1,128]{2,1,0:T(1,128)S(1)}, f32[10,1,128]{2,1,0:T(1,128)S(1)}, u32[]{:S(2)}, u32[]{:S(2)}) collective-permute-start(f32[10,1,128]{2,1,0:T(1,128)S(1)} %get-tuple-element.29), channel_id=1, source_target_pairs={{0,1},{1,2},{2,3},{3,4},{4,5},{5,6},{6,7},{8,9},{9,10},{10,11},{11... | collective-permute-start | bytes 15368 | tf_op jit(solution)/shard_map/ppermute | solution.py:14
  13.6 8.0 %collective-permute-start.4 = (f32[10,1,128]{2,1,0:T(1,128)S(1)}, f32[10,1,128]{2,1,0:T(1,128)S(1)}, u32[]{:S(2)}, u32[]{:S(2)}) collective-permute-start(f32[10,1,128]{2,1,0:T(1,128)S(1)} %get-tuple-element.30), channel_id=1, source_target_pairs={{1,0},{2,1},{3,2},{4,3},{5,4},{6,5},{7,6},{9,8},{10,9},{11,10},{12... | collective-permute-start | bytes 15368 | tf_op jit(solution)/shard_map/ppermute | solution.py:15
  15.6 7.6 %collective-permute-start.1 = (f32[3,1,8,128]{3,2,1,0:T(8,128)S(1)}, f32[3,1,8,128]{3,2,1,0:T(8,128)S(1)}, u32[]{:S(2)}, u32[]{:S(2)}) collective-permute-start(f32[3,1,8,128]{3,2,1,0:T(8,128)S(1)} %get-tuple-element.25), channel_id=1, source_target_pairs={{8,0},{16,8},{24,16},{9,1},{17,9},{25,17},{10,2},{18,10},{26,18},{... | collective-permute-start | bytes 36872 | tf_op jit(solution)/shard_map/ppermute | solution.py:15
  16.9 5.4 %collective-permute-start.3 = (f32[3,1,8,128]{3,2,1,0:T(8,128)S(1)}, f32[3,1,8,128]{3,2,1,0:T(8,128)S(1)}, u32[]{:S(2)}, u32[]{:S(2)}) collective-permute-start(f32[3,1,8,128]{3,2,1,0:T(8,128)S(1)} %get-tuple-element.26), channel_id=1, source_target_pairs={{0,8},{8,16},{16,24},{1,9},{9,17},{17,25},{2,10},{10,18},{18,26},{... | collective-permute-start | bytes 36872 | tf_op jit(solution)/shard_map/ppermute | solution.py:14
  23.3 6.4 %collective-permute-start.7 = (f32[3,10,1,128]{3,2,1,0:T(1,128)S(1)}, f32[3,10,1,128]{3,2,1,0:T(1,128)S(1)}, u32[]{:S(2)}, u32[]{:S(2)}) collective-permute-start(f32[3,10,1,128]{3,2,1,0:T(1,128)S(1)} %get-tuple-element.17), channel_id=1, source_target_pairs={{0,1},{1,2},{2,3},{3,4},{4,5},{5,6},{6,7},{8,9},{9,10},{10,11},{11... | collective-permute-start | bytes 46088 | tf_op jit(solution)/shard_map/ppermute | solution.py:14
  27.6 6.1 %collective-permute-start.5 = (f32[3,10,1,128]{3,2,1,0:T(1,128)S(1)}, f32[3,10,1,128]{3,2,1,0:T(1,128)S(1)}, u32[]{:S(2)}, u32[]{:S(2)}) collective-permute-start(f32[3,10,1,128]{3,2,1,0:T(1,128)S(1)} %get-tuple-element.18), channel_id=1, source_target_pairs={{1,0},{2,1},{3,2},{4,3},{5,4},{6,5},{7,6},{9,8},{10,9},{11,10},{12... | collective-permute-start | bytes 46088 | tf_op jit(solution)/shard_map/ppermute | solution.py:15
  35.2 3.8 %collective-permute-start.9 = (f32[3,1,8,128]{3,2,1,0:T(8,128)S(1)}, f32[3,1,8,128]{3,2,1,0:T(8,128)S(1)}, u32[]{:S(2)}, u32[]{:S(2)}) collective-permute-start(f32[3,1,8,128]{3,2,1,0:T(8,128)S(1)} %get-tuple-element.23), channel_id=1, source_target_pairs={{0,8},{8,16},{16,24},{1,9},{9,17},{17,25},{2,10},{10,18},{18,26},{... | collective-permute-start | bytes 36872 | tf_op jit(solution)/shard_map/ppermute | solution.py:14
  37.7 6.0 %collective-permute-start.8 = (f32[3,1,8,128]{3,2,1,0:T(8,128)S(1)}, f32[3,1,8,128]{3,2,1,0:T(8,128)S(1)}, u32[]{:S(2)}, u32[]{:S(2)}) collective-permute-start(f32[3,1,8,128]{3,2,1,0:T(8,128)S(1)} %get-tuple-element.24), channel_id=1, source_target_pairs={{8,0},{16,8},{24,16},{9,1},{17,9},{25,17},{10,2},{18,10},{26,18},{... | collective-permute-start | bytes 36872 | tf_op jit(solution)/shard_map/ppermute | solution.py:15
  43.7 6.2 %collective-permute-start.11 = (f32[3,10,1,128]{3,2,1,0:T(1,128)S(1)}, f32[3,10,1,128]{3,2,1,0:T(1,128)S(1)}, u32[]{:S(2)}, u32[]{:S(2)}) collective-permute-start(f32[3,10,1,128]{3,2,1,0:T(1,128)S(1)} %get-tuple-element.15), channel_id=1, source_target_pairs={{0,1},{1,2},{2,3},{3,4},{4,5},{5,6},{6,7},{8,9},{9,10},{10,11},{11... | collective-permute-start | bytes 46088 | tf_op jit(solution)/shard_map/ppermute | solution.py:14
  48.6 5.6 %collective-permute-start.10 = (f32[3,10,1,128]{3,2,1,0:T(1,128)S(1)}, f32[3,10,1,128]{3,2,1,0:T(1,128)S(1)}, u32[]{:S(2)}, u32[]{:S(2)}) collective-permute-start(f32[3,10,1,128]{3,2,1,0:T(1,128)S(1)} %get-tuple-element.16), channel_id=1, source_target_pairs={{1,0},{2,1},{3,2},{4,3},{5,4},{6,5},{7,6},{9,8},{10,9},{11,10},{12... | collective-permute-start | bytes 46088 | tf_op jit(solution)/shard_map/ppermute | solution.py:15
  55.6 4.2 %collective-permute-start.13 = (f32[3,1,8,128]{3,2,1,0:T(8,128)S(1)}, f32[3,1,8,128]{3,2,1,0:T(8,128)S(1)}, u32[]{:S(2)}, u32[]{:S(2)}) collective-permute-start(f32[3,1,8,128]{3,2,1,0:T(8,128)S(1)} %get-tuple-element.21), channel_id=1, source_target_pairs={{0,8},{8,16},{16,24},{1,9},{9,17},{17,25},{2,10},{10,18},{18,26},{... | collective-permute-start | bytes 36872 | tf_op jit(solution)/shard_map/ppermute | solution.py:14
  58.5 4.0 %collective-permute-start.12 = (f32[3,1,8,128]{3,2,1,0:T(8,128)S(1)}, f32[3,1,8,128]{3,2,1,0:T(8,128)S(1)}, u32[]{:S(2)}, u32[]{:S(2)}) collective-permute-start(f32[3,1,8,128]{3,2,1,0:T(8,128)S(1)} %get-tuple-element.22), channel_id=1, source_target_pairs={{8,0},{16,8},{24,16},{9,1},{17,9},{25,17},{10,2},{18,10},{26,18},{... | collective-permute-start | bytes 36872 | tf_op jit(solution)/shard_map/ppermute | solution.py:15
  62.5 4.4 %collective-permute-start.15 = (f32[3,10,1,128]{3,2,1,0:T(1,128)S(1)}, f32[3,10,1,128]{3,2,1,0:T(1,128)S(1)}, u32[]{:S(2)}, u32[]{:S(2)}) collective-permute-start(f32[3,10,1,128]{3,2,1,0:T(1,128)S(1)} %get-tuple-element.13), channel_id=1, source_target_pairs={{0,1},{1,2},{2,3},{3,4},{4,5},{5,6},{6,7},{8,9},{9,10},{10,11},{11... | collective-permute-start | bytes 46088 | tf_op jit(solution)/shard_map/ppermute | solution.py:14
  65.5 5.6 %collective-permute-start.14 = (f32[3,10,1,128]{3,2,1,0:T(1,128)S(1)}, f32[3,10,1,128]{3,2,1,0:T(1,128)S(1)}, u32[]{:S(2)}, u32[]{:S(2)}) collective-permute-start(f32[3,10,1,128]{3,2,1,0:T(1,128)S(1)} %get-tuple-element.14), channel_id=1, source_target_pairs={{1,0},{2,1},{3,2},{4,3},{5,4},{6,5},{7,6},{9,8},{10,9},{11,10},{12... | collective-permute-start | bytes 46088 | tf_op jit(solution)/shard_map/ppermute | solution.py:15
  72.5 4.5 %collective-permute-start.17 = (f32[3,1,8,128]{3,2,1,0:T(8,128)S(1)}, f32[3,1,8,128]{3,2,1,0:T(8,128)S(1)}, u32[]{:S(2)}, u32[]{:S(2)}) collective-permute-start(f32[3,1,8,128]{3,2,1,0:T(8,128)S(1)} %get-tuple-element.19), channel_id=1, source_target_pairs={{0,8},{8,16},{16,24},{1,9},{9,17},{17,25},{2,10},{10,18},{18,26},{... | collective-permute-start | bytes 36872 | tf_op jit(solution)/shard_map/ppermute | solution.py:14
  75.7 3.8 %collective-permute-start.16 = (f32[3,1,8,128]{3,2,1,0:T(8,128)S(1)}, f32[3,1,8,128]{3,2,1,0:T(8,128)S(1)}, u32[]{:S(2)}, u32[]{:S(2)}) collective-permute-start(f32[3,1,8,128]{3,2,1,0:T(8,128)S(1)} %get-tuple-element.20), channel_id=1, source_target_pairs={{8,0},{16,8},{24,16},{9,1},{17,9},{25,17},{10,2},{18,10},{26,18},{... | collective-permute-start | bytes 36872 | tf_op jit(solution)/shard_map/ppermute | solution.py:15
  79.5 13.4 %collective-permute-start.19 = (f32[3,10,1,128]{3,2,1,0:T(1,128)S(1)}, f32[3,10,1,128]{3,2,1,0:T(1,128)S(1)}, u32[]{:S(2)}, u32[]{:S(2)}) collective-permute-start(f32[3,10,1,128]{3,2,1,0:T(1,128)S(1)} %get-tuple-element.11), channel_id=1, source_target_pairs={{0,1},{1,2},{2,3},{3,4},{4,5},{5,6},{6,7},{8,9},{9,10},{10,11},{11... | collective-permute-start | bytes 46088 | tf_op jit(solution)/shard_map/ppermute | solution.py:14
  84.3 8.6 %collective-permute-start.18 = (f32[3,10,1,128]{3,2,1,0:T(1,128)S(1)}, f32[3,10,1,128]{3,2,1,0:T(1,128)S(1)}, u32[]{:S(2)}, u32[]{:S(2)}) collective-permute-start(f32[3,10,1,128]{3,2,1,0:T(1,128)S(1)} %get-tuple-element.12), channel_id=1, source_target_pairs={{1,0},{2,1},{3,2},{4,3},{5,4},{6,5},{7,6},{9,8},{10,9},{11,10},{12... | collective-permute-start | bytes 46088 | tf_op jit(solution)/shard_map/ppermute | solution.py:15
  94.3 17.7 %copy-start.1 = (f32[3,8,8,128]{3,2,1,0:T(8,128)}, f32[3,8,8,128]{3,2,1,0:T(8,128)S(1)}, u32[]{:S(2)}) copy-start(f32[3,8,8,128]{3,2,1,0:T(8,128)S(1)} %fusion.7) | copy-start | bytes 294916
